TPU v7x, 32 devices: a whole 2x2x4 slice. The times are simulated.
32 devices in a mesh: group: 2 (over y), seq: 4 (over z), head: 2 (over x), rep: 2 (over core).
Axes of the slice: x: 2, y: 2, z: 4, core: 2. Of those that a mesh axis runs over, the one named last changes fastest.
Arguments:
- span_q: bfloat16 [8, 128, 8192], P('group', 'seq', ('head', 'rep')), parts along dimension 0, may hold values from -144 to 144
- span_raw_keys: bfloat16 [8, 128, 1024], P('group', 'seq', 'head'), parts along dimension 0, may hold values from -6 to 6
- span_raw_values: bfloat16 [8, 128, 1024], P('group', 'seq', 'head'), parts along dimension 0, may hold values from -6 to 6
- prompt_cache_keys: bfloat16 [8, 256, 1024], P('group', 'seq', 'head'), parts along dimension 0, may hold values from -6 to 6
- prompt_cache_values: bfloat16 [8, 256, 1024], P('group', 'seq', 'head'), parts along dimension 0, may hold values from -6 to 6
- span_offsets: int32 [8], P('group'), parts along dimension 0, may hold values from 1 to 256
- decode_new_queries: bfloat16 [64, 4, 8192], P(('group', 'seq'), None, ('head', 'rep')), parts along dimension 0, may hold values from -144 to 144
- decode_new_keys: bfloat16 [64, 4, 1024], P(('group', 'seq'), None, 'head'), parts along dimension 0, may hold values from -6 to 6
- decode_new_values: bfloat16 [64, 4, 1024], P(('group', 'seq'), None, 'head'), parts along dimension 0, may hold values from -6 to 6
- generated_keys: bfloat16 [64, 128, 1024], P(('group', 'seq'), None, 'head'), parts along dimension 0, may hold values from -6 to 6
- generated_values: bfloat16 [64, 128, 1024], P(('group', 'seq'), None, 'head'), parts along dimension 0, may hold values from -6 to 6
- row_request: int32 [64], P(('group', 'seq')), parts along dimension 0, may hold values from 0 to 3
- row_length: int32 [64], P(('group', 'seq')), parts along dimension 0, may hold values from 1 to 128
Outputs:
- span_output: bfloat16 [8, 128, 8192], P('group', 'seq', ('head', 'rep')), parts along dimension 0
- dec_out: bfloat16 [64, 4, 8192], P(('group', 'seq'), None, ('head', 'rep')), parts along dimension 0
There are 2 independent parts, one for each index of `group`. A program takes and returns all parts, laid end to end along the dimension named above; each array names one. Nothing has to cross between parts.
All inputs are finite; a program needn't handle non-finite values.
Results may differ from a plain program's by a relative error of at most 0.012.
Values may be sent and summed in bfloat16 or wider, within the bound.
No kernel may reach another device: no remote copies, remote signals or barrier semaphores. Data moves between devices by JAX's collectives and lax.ppermute only.
A program may use at most 64 MiB of HBM per device.

v0:
```python
import functools
import math

import jax
import jax.numpy as jnp
from jax import lax
from jax.experimental import pallas as pl
from jax.experimental.pallas import tpu as pltpu
from jax.sharding import PartitionSpec as P

QUERY_HEADS = 64
KEY_VALUE_HEADS = 8
HEAD_WIDTH = 128
HALF = HEAD_WIDTH // 2
GROUPS = QUERY_HEADS // KEY_VALUE_HEADS

very_low = -1e30
RATE = HEAD_WIDTH ** (-0.5) * math.log2(math.e)
HBM = pl.BlockSpec(memory_space=pltpu.HBM)
SMEM = pl.BlockSpec(memory_space=pltpu.SMEM)
VMEM = pl.BlockSpec(memory_space=pltpu.VMEM)
bf16 = jnp.bfloat16
f32 = jnp.float32


def tile(n):
    return pl.ds(n * HEAD_WIDTH, HEAD_WIDTH)


def iota(shape, axis):
    return lax.broadcasted_iota(jnp.int32, shape, axis)


def angle_tables(positions):
    lane = iota(positions.shape, 1)
    freqs = jnp.exp((lane % HALF).astype(f32) * (-2.0 * math.log(500000.0) / HEAD_WIDTH))
    angles = positions.astype(f32) * freqs
    return jnp.cos(angles), jnp.sin(angles)


def signed(sine):
    return jnp.where(iota(sine.shape, 1) < HALF, -sine, sine)


def rotate(x, cosine, sine):
    return x * cosine + pltpu.roll(x, HALF, axis=1) * sine


def token_tables(table, ch, row):
    cos_t, sin_t = table[0, pl.ds(0, ch), :], table[1, pl.ds(0, ch), :]
    cos_b, sin_b = table[0, pl.ds(row, 1), :], table[1, pl.ds(row, 1), :]
    return cos_b * cos_t - sin_b * sin_t, signed(sin_b * cos_t + cos_b * sin_t)


def first_head(q_heads, kv_local):
    block = lax.axis_index("head") * lax.axis_size("rep") + lax.axis_index("rep")
    return block * q_heads // GROUPS - lax.axis_index("head") * kv_local


def dot_nt(a, b):
    return lax.dot_general(a, b, (((1,), (1,)), ((), ())), preferred_element_type=f32)


def dot_tn(a, b):
    return lax.dot_general(a, b, (((0,), (0,)), ((), ())), preferred_element_type=f32)


def by_row(ref, lanes, step_rows, lookup=None):
    row = iota((1, lanes), 1) // step_rows
    out = jnp.zeros((1, lanes), jnp.int32)
    for r in range(lanes // step_rows):
        value = ref[r] if lookup is None else lookup[ref[r]]
        out = jnp.where(row == r, value, out)
    return out


def pack_keys_kernel(q_heads, kv_local, used, cache_ref, span_ref, out_ref, sem):
    prompts, pre, _ = cache_ref.shape
    ch = span_ref.shape[1]
    first = first_head(q_heads, kv_local)
    copies = []
    for p in range(prompts):
        for h in range(used):
            lanes = pl.ds(pl.multiple_of((first + h) * HEAD_WIDTH, HEAD_WIDTH), HEAD_WIDTH)
            for j, ref, rows in ((0, cache_ref, pl.ds(0, pre)), (1, span_ref, pl.ds(pre, ch))):
                copies.append(
                    pltpu.make_async_copy(
                        ref.at[p, :, lanes],
                        out_ref.at[rows, tile(h * prompts + p)],
                        sem.at[p, h, j],
                    )
                )
    for copy in copies:
        copy.start()
    for copy in copies:
        copy.wait()


def pack_values_kernel(q_heads, kv_local, used, cache_ref, span_ref, out_ref, sem):
    prompts, pre, _ = cache_ref.shape
    ch = span_ref.shape[1]
    first = first_head(q_heads, kv_local)
    lanes = pl.ds(pl.multiple_of(first * HEAD_WIDTH, HEAD_WIDTH), used * HEAD_WIDTH)
    copies = []
    for p in range(prompts):
        for j, ref, start, size in ((0, cache_ref, 0, pre), (1, span_ref, pre, ch)):
            copies.append(
                pltpu.make_async_copy(
                    ref.at[p, :, lanes],
                    out_ref.at[pl.ds(p * (pre + ch) + start, size), :],
                    sem.at[p, j],
                )
            )
    for copy in copies:
        copy.start()
    for copy in copies:
        copy.wait()


def prepare_kernel(
    shards,
    q_heads,
    kv_local,
    used,
    per_kv,
    begin_ref,
    request_ref,
    length_ref,
    span_q_ref,
    dec_q_ref,
    new_k_ref,
    new_v_ref,
    gen_k_ref,
    gen_v_ref,
    table_ref,
    q_ref,
    q_cat_ref,
    acc_ref,
    stat_ref,
    gk_scr,
    gv_scr,
    q_scr,
    n_scr,
    sem,
):
    prompts, ch, _ = span_q_ref.shape
    rows_local, steps, _ = dec_q_ref.shape
    gen = gen_k_ref.shape[1]
    step_rows = per_kv * steps
    dec_rows = rows_local * step_rows
    first = first_head(q_heads, kv_local)
    lanes = pl.ds(pl.multiple_of(first * HEAD_WIDTH, HEAD_WIDTH), used * HEAD_WIDTH)
    copies = [
        pltpu.make_async_copy(src.at[:, :, lanes], dst, sem.at[i])
        for i, (src, dst) in enumerate(((gen_k_ref, gk_scr), (gen_v_ref, gv_scr)))
    ]
    for copy in copies:
        copy.start()

    me = lax.axis_index("seq")
    base_rows = prompts * shards
    count = table_ref.shape[1]
    position = iota((count, HEAD_WIDTH), 0)
    for p in range(prompts):
        start = ch + p * shards
        row = iota((count, HEAD_WIDTH), 0)
        here = (row >= start) & (row < start + shards)
        position = jnp.where(here, begin_ref[p] + (row - start) * ch, position)
    for r in range(rows_local):
        start = ch + base_rows + r * steps
        row = iota((count, HEAD_WIDTH), 0)
        here = (row >= start) & (row < start + steps)
        length = begin_ref[request_ref[r]] + ch * shards + length_ref[r]
        position = jnp.where(here, length + row - start, position)
    cosine, sine = angle_tables(position)
    table_ref[0] = cosine
    table_ref[1] = sine

    for p in range(prompts):
        cosine, sine = token_tables(table_ref, ch, ch + p * shards + me)
        for h in range(used):
            for g in range(per_kv):
                x = span_q_ref[p, :, tile(h * per_kv + g)].astype(f32)
                q_ref[p, h, pl.ds(g * ch, ch), :] = rotate(x, cosine, sine).astype(bf16)

    n_scr[...] = jnp.zeros_like(n_scr)
    pad = n_scr.shape[2]
    for r in range(rows_local):
        rows = pl.ds(ch + base_rows + r * steps, steps)
        cosine = table_ref[0, rows, :]
        sine = signed(table_ref[1, rows, :])
        for h in range(used):
            for g in range(per_kv):
                x = dec_q_ref[r, :, tile(h * per_kv + g)].astype(f32)
                q_scr[h, pl.ds(r * step_rows + g * steps, steps), :] = rotate(x, cosine, sine)
            own = pl.ds(pl.multiple_of((first + h) * HEAD_WIDTH, HEAD_WIDTH), HEAD_WIDTH)
            n_scr[0, r * used + h, pl.ds(0, steps), :] = rotate(
                new_k_ref[r, :, own].astype(f32), cosine, sine
            )
            n_scr[1, r * used + h, pl.ds(0, steps), :] = new_v_ref[r, :, own].astype(f32)

    for h in range(used):
        for r in range(rows_local):
            rows = pl.ds(r * step_rows, step_rows)
            x = q_scr[h, rows, :]
            for p in range(prompts):
                q_cat_ref[h, rows, tile(p)] = jnp.where(request_ref[r] == p, x, 0.0).astype(bf16)

    for copy in copies:
        copy.wait()
    span = min(HEAD_WIDTH, dec_rows)
    group = span // step_rows
    lengths = by_row(length_ref, dec_rows, step_rows)
    begins = by_row(request_ref, dec_rows, step_rows, begin_ref)
    requests = by_row(request_ref, dec_rows, step_rows)
    key = iota((gen + pad, span), 0)
    lane = iota((gen + pad, span), 1)
    new_seen = (key >= gen) & (key - gen <= lane % steps)
    for h in range(used):
        stat_ref[h, pl.ds(2, 1), :] = begins.astype(f32)
        stat_ref[h, pl.ds(3, 1), :] = requests.astype(f32)
        for i in range(dec_rows // span):
            cols = pl.ds(i * span, span)
            q = q_scr[h, cols, :].astype(bf16)
            row = iota((span, HEAD_WIDTH), 0) // step_rows
            scores = None
            for j in range(group):
                r = i * group + j
                keys = jnp.concatenate(
                    [gk_scr[r, :, tile(h)], n_scr[0, r * used + h].astype(bf16)], axis=0
                )
                part = dot_nt(keys, jnp.where(row == j, q, jnp.zeros_like(q)))
                scores = part if scores is None else scores + part
            seen = (key < lengths[:, i * span : (i + 1) * span]) | new_seen
            scores = jnp.where(seen, scores, very_low)
            top = jnp.max(scores, axis=0, keepdims=True)
            weights = jnp.exp2((scores - top) * RATE)
            total = jnp.sum(weights, axis=0, keepdims=True)
            acc = None
            for j in range(group):
                r = i * group + j
                values = jnp.concatenate(
                    [gv_scr[r, :, tile(h)], n_scr[1, r * used + h].astype(bf16)], axis=0
                )
                part = dot_tn(
                    values, jnp.where(lane // step_rows == j, weights, 0.0).astype(bf16)
                )
                acc = part if acc is None else acc + part
            acc_ref[h, :, cols] = acc
            stat_ref[h, pl.ds(0, 1), cols] = top
            stat_ref[h, pl.ds(1, 1), cols] = total


def rotate_keys(chunk_ref, k_scr, table_ref, shards, prompts, used, pre, ch, shard, at):
    k_scr[pl.ds(at, pre), :] = chunk_ref[pl.ds(0, pre), :]
    for p in range(prompts):
        cosine, sine = token_tables(table_ref, ch, ch + p * shards + shard)
        for h in range(used):
            lanes = tile(h * prompts + p)
            x = chunk_ref[pl.ds(pre, ch), lanes].astype(f32)
            k_scr[pl.ds(at + pre, ch), lanes] = rotate(x, cosine, sine).astype(bf16)


def hide(scores, pre, begin, last):
    n, lanes = scores.shape
    low = scores[:pre]
    low = jnp.where(iota(low.shape, 0) < begin, low, very_low)
    high = scores[pre:]
    if last is not None:
        high = jnp.where(iota(high.shape, 0) <= last, high, very_low)
    return jnp.concatenate([low, high], axis=0)


def masked_stack(weights, requests, prompts):
    return jnp.concatenate(
        [jnp.where(requests == p, weights, 0.0).astype(bf16) for p in range(prompts)], axis=0
    )


def near_kernel(shards, used, ch, count, *refs):
    begin_ref = refs[0]
    keys, values = refs[1 : 1 + count], refs[1 + count : 1 + 2 * count]
    table_ref, q_ref, q_cat_ref, acc_in_ref, stat_in_ref = refs[1 + 2 * count : 6 + 2 * count]
    acc_ref, stat_ref, dec_acc_ref, dec_stat_ref, k_scr = refs[6 + 2 * count :]
    prompts, _, rows, _ = q_ref.shape
    size = keys[0].shape[0]
    dec_rows = q_cat_ref.shape[1]
    me = lax.axis_index("seq")
    pre = size - ch
    shard = [lax.rem(me + shards - c, shards) for c in range(count)]
    for c in range(count):
        rotate_keys(
            keys[c], k_scr, table_ref, shards, prompts, used, pre, ch, shard[c], c * size
        )
    token = me * ch + iota((1, rows), 1) % ch
    for h in range(used):
        requests = stat_in_ref[h, pl.ds(3, 1), :]
        begins = stat_in_ref[h, pl.ds(2, 1), :].astype(jnp.int32)
        for p in range(prompts):
            pieces = []
            for c in range(count):
                k = k_scr[pl.ds(c * size, size), tile(h * prompts + p)]
                pieces.append(
                    hide(
                        dot_nt(k, q_ref[p, h]),
                        pre,
                        begin_ref[p] - shard[c] * pre,
                        token - shard[c] * ch,
                    )
                )
            scores = jnp.concatenate(pieces, axis=0)
            top = jnp.max(scores, axis=0, keepdims=True)
            weights = jnp.exp2((scores - top) * RATE)
            total = jnp.sum(weights, axis=0, keepdims=True)
            v = jnp.concatenate(
                [ref[pl.ds(p * size, size), tile(h)] for ref in values], axis=0
            )
            acc_ref[p, h] = dot_tn(v, weights.astype(bf16))
            stat_ref[p, h, pl.ds(0, 1), :] = top
            stat_ref[p, h, pl.ds(1, 1), :] = total

        pieces = []
        for c in range(count):
            k = k_scr[pl.ds(c * size, size), pl.ds(h * prompts * HEAD_WIDTH, prompts * HEAD_WIDTH)]
            pieces.append(hide(dot_nt(k, q_cat_ref[h]), pre, begins - shard[c] * pre, None))
        scores = jnp.concatenate(pieces, axis=0)
        old_top = stat_in_ref[h, pl.ds(0, 1), :]
        top = jnp.maximum(jnp.max(scores, axis=0, keepdims=True), old_top)
        factor = jnp.exp2((old_top - top) * RATE)
        weights = jnp.exp2((scores - top) * RATE)
        total = jnp.sum(weights, axis=0, keepdims=True) + stat_in_ref[h, pl.ds(1, 1), :] * factor
        acc = acc_in_ref[h] * factor
        for c in range(count):
            w = masked_stack(weights[c * size : (c + 1) * size], requests, prompts)
            acc = acc + dot_tn(values[c][:, tile(h)], w)
        dec_acc_ref[h] = acc
        dec_stat_ref[h, pl.ds(0, 1), :] = top
        dec_stat_ref[h, pl.ds(1, 1), :] = total
        dec_stat_ref[h, pl.ds(2, 2), :] = stat_in_ref[h, pl.ds(2, 2), :]


def far_kernel(
    shards,
    used,
    ch,
    begin_ref,
    key_ref,
    table_ref,
    q_ref,
    q_cat_ref,
    acc_ref,
    stat_ref,
    dec_acc_ref,
    dec_stat_ref,
    base_ref,
    weight_ref,
    dec_base_ref,
    dec_weight_ref,
    k_scr,
):
    prompts, _, rows, _ = q_ref.shape
    size = key_ref.shape[0]
    me = lax.axis_index("seq")
    pre = size - ch
    shard = lax.rem(me + 1, shards)
    rotate_keys(key_ref, k_scr, table_ref, shards, prompts, used, pre, ch, shard, 0)
    token = me * ch + iota((1, rows), 1) % ch

    def finish(scores, old_top, old_total, old_acc):
        top = jnp.maximum(jnp.max(scores, axis=0, keepdims=True), old_top)
        factor = jnp.exp2((old_top - top) * RATE)
        weights = jnp.exp2((scores - top) * RATE)
        total = jnp.sum(weights, axis=0, keepdims=True) + old_total * factor
        inverse = 1.0 / total
        return weights * inverse, old_acc * (factor * inverse)

    for h in range(used):
        for p in range(prompts):
            scores = hide(
                dot_nt(k_scr[:, tile(h * prompts + p)], q_ref[p, h]),
                pre,
                begin_ref[p] - shard * pre,
                token - shard * ch,
            )
            weights, base = finish(
                scores, stat_ref[p, h, pl.ds(0, 1), :], stat_ref[p, h, pl.ds(1, 1), :], acc_ref[p, h]
            )
            weight_ref[p, h] = weights.T.astype(bf16)
            base_ref[p, h] = base.T
        begins = dec_stat_ref[h, pl.ds(2, 1), :].astype(jnp.int32)
        requests = dec_stat_ref[h, pl.ds(3, 1), :]
        k = k_scr[:, pl.ds(h * prompts * HEAD_WIDTH, prompts * HEAD_WIDTH)]
        scores = hide(dot_nt(k, q_cat_ref[h]), pre, begins - shard * pre, None)
        weights, base = finish(
            scores, dec_stat_ref[h, pl.ds(0, 1), :], dec_stat_ref[h, pl.ds(1, 1), :], dec_acc_ref[h]
        )
        stack = jnp.concatenate(
            [jnp.where(requests == p, weights, 0.0) for p in range(prompts)], axis=0
        )
        dec_weight_ref[h] = stack.T.astype(bf16)
        dec_base_ref[h] = base.T


def last_kernel(
    used,
    per_kv,
    steps,
    value_ref,
    base_ref,
    weight_ref,
    dec_base_ref,
    dec_weight_ref,
    span_ref,
    dec_ref,
    span_scr,
    dec_scr,
    sem,
):
    prompts, _, rows, size = weight_ref.shape
    ch = rows // per_kv
    step_rows = per_kv * steps
    copies = []
    for p in range(prompts):
        for h in range(used):
            out = base_ref[p, h] + jnp.dot(
                weight_ref[p, h],
                value_ref[pl.ds(p * size, size), tile(h)],
                preferred_element_type=f32,
            )
            out = out.astype(bf16)
            for g in range(per_kv):
                span_scr[p, :, tile(h * per_kv + g)] = out[g * ch : (g + 1) * ch]
        copies.append(pltpu.make_async_copy(span_scr.at[p], span_ref.at[p], sem.at[p]))
        copies[-1].start()
    for h in range(used):
        out = dec_base_ref[h] + jnp.dot(
            dec_weight_ref[h], value_ref[:, tile(h)], preferred_element_type=f32
        )
        for r in range(dec_scr.shape[0]):
            for g in range(per_kv):
                start = r * step_rows + g * steps
                dec_scr[r, :, tile(h * per_kv + g)] = out[start : start + steps].astype(bf16)
    copies.append(pltpu.make_async_copy(dec_scr, dec_ref, sem.at[prompts]))
    copies[-1].start()
    for copy in copies:
        copy.wait()


def body(
    span_q,
    span_raw_keys,
    span_raw_values,
    prompt_cache_keys,
    prompt_cache_values,
    span_offsets,
    decode_new_queries,
    decode_new_keys,
    decode_new_values,
    generated_keys,
    generated_values,
    row_request,
    row_length,
):
    prompts, ch, q_width = span_q.shape
    pre = prompt_cache_keys.shape[1]
    q_heads = q_width // HEAD_WIDTH
    kv_local = span_raw_keys.shape[2] // HEAD_WIDTH
    used = max(1, q_heads // GROUPS)
    per_kv = q_heads // used
    width = used * HEAD_WIDTH
    shards = lax.axis_size("seq")
    rows_local, steps = decode_new_queries.shape[:2]
    gen = generated_keys.shape[1]
    step_rows = per_kv * steps
    dec_rows = rows_local * step_rows
    rows = per_kv * ch
    size = pre + ch
    params = functools.partial(pltpu.CompilerParams, vmem_limit_bytes=16 << 20)
    shape = jax.ShapeDtypeStruct

    own_keys = pl.pallas_call(
        functools.partial(pack_keys_kernel, q_heads, kv_local, used),
        out_shape=shape((size, prompts * width), bf16),
        in_specs=[HBM, HBM],
        out_specs=VMEM,
        scratch_shapes=[pltpu.SemaphoreType.DMA((prompts, used, 2))],
        compiler_params=params(),
        name="pack_keys",
    )(prompt_cache_keys, span_raw_keys)
    own_values = pl.pallas_call(
        functools.partial(pack_values_kernel, q_heads, kv_local, used),
        out_shape=shape((prompts * size, width), bf16),
        in_specs=[HBM, HBM],
        out_specs=VMEM,
        scratch_shapes=[pltpu.SemaphoreType.DMA((prompts, 2))],
        compiler_params=params(),
        name="pack_values",
    )(prompt_cache_values, span_raw_values)

    ring = [(i, (i + 1) % shards) for i in range(shards)]
    keys = [own_keys]
    values = [own_values]
    for _ in range(shards - 1):
        keys.append(lax.ppermute(keys[-1], "seq", ring))
        values.append(lax.ppermute(values[-1], "seq", ring))

    table_rows = -(-(ch + prompts * shards + rows_local * steps) // 8) * 8
    table, queries, dec_queries, gen_acc, gen_stat = pl.pallas_call(
        functools.partial(prepare_kernel, shards, q_heads, kv_local, used, per_kv),
        out_shape=[
            shape((2, table_rows, HEAD_WIDTH), f32),
            shape((prompts, used, rows, HEAD_WIDTH), bf16),
            shape((used, dec_rows, prompts * HEAD_WIDTH), bf16),
            shape((used, HEAD_WIDTH, dec_rows), f32),
            shape((used, 8, dec_rows), f32),
        ],
        in_specs=[SMEM] * 3 + [VMEM] * 4 + [HBM] * 2,
        out_specs=[VMEM] * 5,
        scratch_shapes=[
            pltpu.VMEM((rows_local, gen, width), bf16),
            pltpu.VMEM((rows_local, gen, width), bf16),
            pltpu.VMEM((used, dec_rows, HEAD_WIDTH), f32),
            pltpu.VMEM((2, rows_local * used, 16, HEAD_WIDTH), f32),
            pltpu.SemaphoreType.DMA((2,)),
        ],
        compiler_params=params(),
        name="prepare",
    )(
        span_offsets,
        row_request,
        row_length,
        span_q,
        decode_new_queries,
        decode_new_keys,
        decode_new_values,
        generated_keys,
        generated_values,
    )

    count = shards - 1
    state = [
        shape((prompts, used, HEAD_WIDTH, rows), f32),
        shape((prompts, used, 8, rows), f32),
        shape((used, HEAD_WIDTH, dec_rows), f32),
        shape((used, 8, dec_rows), f32),
    ]
    near = pl.pallas_call(
        functools.partial(near_kernel, shards, used, ch, count),
        out_shape=state,
        in_specs=[SMEM] + [VMEM] * (2 * count + 5),
        out_specs=[VMEM] * 4,
        scratch_shapes=[pltpu.VMEM((count * size, prompts * width), bf16)],
        compiler_params=params(),
        name="near",
    )(span_offsets, *keys[:-1], *values[:-1], table, queries, dec_queries, gen_acc, gen_stat)

    far = pl.pallas_call(
        functools.partial(far_kernel, shards, used, ch),
        out_shape=[
            shape((prompts, used, rows, HEAD_WIDTH), f32),
            shape((prompts, used, rows, size), bf16),
            shape((used, dec_rows, HEAD_WIDTH), f32),
            shape((used, dec_rows, prompts * size), bf16),
        ],
        in_specs=[SMEM] + [VMEM] * 8,
        out_specs=[VMEM] * 4,
        scratch_shapes=[pltpu.VMEM((size, prompts * width), bf16)],
        compiler_params=params(),
        name="far",
    )(span_offsets, keys[-1], table, queries, dec_queries, *near)

    return tuple(
        pl.pallas_call(
            functools.partial(last_kernel, used, per_kv, steps),
            out_shape=[
                shape(span_q.shape, bf16),
                shape(decode_new_queries.shape, bf16),
            ],
            in_specs=[VMEM] * 5,
            out_specs=[HBM, HBM],
            scratch_shapes=[
                pltpu.VMEM(span_q.shape, bf16),
                pltpu.VMEM(decode_new_queries.shape, bf16),
                pltpu.SemaphoreType.DMA((prompts + 1,)),
            ],
            compiler_params=params(),
            name="last",
        )(values[-1], *far)
    )


def solution(mesh):
    in_specs = (
        P("group", "seq", ("head", "rep")),
        P("group", "seq", "head"),
        P("group", "seq", "head"),
        P("group", "seq", "head"),
        P("group", "seq", "head"),
        P("group"),
        P(("group", "seq"), None, ("head", "rep")),
        P(("group", "seq"), None, "head"),
        P(("group", "seq"), None, "head"),
        P(("group", "seq"), None, "head"),
        P(("group", "seq"), None, "head"),
        P(("group", "seq")),
        P(("group", "seq")),
    )
    out_specs = (P("group", "seq", ("head", "rep")), P(("group", "seq"), None, ("head", "rep")))
    return jax.shard_map(body, mesh=mesh, in_specs=in_specs, out_specs=out_specs, check_vma=False)
```

profile of v0, /device:TPU:0, one launch (start us, length us, event | category | flops | bytes accessed | tf_op | source)
XLA Modules:
  0.0 42.7 jit_solution(15702193662412471697)
XLA Ops:
  0.7 1.0 %copy-done.3 = bf16[4,64,512]{2,1,0:T(8,128)(2,1)S(1)} copy-done((bf16[4,64,512]{2,1,0:T(8,128)(2,1)S(1)}, bf16[4,64,512]{2,1,0:T(8,128)(2,1)}, u32[]{:S(2)}) %copy-start.3) | copy-done | bytes 262168
  1.7 0.9 %copy-done.6 = bf16[4,32,512]{2,1,0:T(8,128)(2,1)S(1)} copy-done((bf16[4,32,512]{2,1,0:T(8,128)(2,1)S(1)}, bf16[4,32,512]{2,1,0:T(8,128)(2,1)}, u32[]{:S(2)}) %copy-start.6) | copy-done | bytes 131096
  2.6 0.2 pack_keys.1.refs_1_
  2.8 3.1 %collective-permute-start.3 = (bf16[96,1024]{1,0:T(8,128)(2,1)S(1)}, bf16[96,1024]{1,0:T(8,128)(2,1)S(1)}, u32[]{:S(2)}, u32[]{:S(2)}) collective-permute-start(bf16[96,1024]{1,0:T(8,128)(2,1)S(1)} %pack_keys.1.refs_1_), channel_id=1, source_target_pairs={{0,4},{4,8},{8,12},{12,0},{1,5},{5,9},{9,13},{13,1},{2,6},{6,10},{... | collective-permute-start | bytes 589832 | tf_op jit(solution)/shard_map/ppermute | solution.py:504
  5.9 0.9 %copy-done.4 = bf16[4,64,512]{2,1,0:T(8,128)(2,1)S(1)} copy-done((bf16[4,64,512]{2,1,0:T(8,128)(2,1)S(1)}, bf16[4,64,512]{2,1,0:T(8,128)(2,1)}, u32[]{:S(2)}) %copy-start.4) | copy-done | bytes 262168
  6.9 0.9 %copy-done.7 = bf16[4,32,512]{2,1,0:T(8,128)(2,1)S(1)} copy-done((bf16[4,32,512]{2,1,0:T(8,128)(2,1)S(1)}, bf16[4,32,512]{2,1,0:T(8,128)(2,1)}, u32[]{:S(2)}) %copy-start.7) | copy-done | bytes 131096
  7.8 0.1 pack_values.1.refs_4_
  7.9 1.6 %collective-permute-start = (bf16[384,256]{1,0:T(8,128)(2,1)S(1)}, bf16[384,256]{1,0:T(8,128)(2,1)S(1)}, u32[]{:S(2)}, u32[]{:S(2)}) collective-permute-start(bf16[384,256]{1,0:T(8,128)(2,1)S(1)} %pack_values.1.refs_4_), channel_id=1, source_target_pairs={{0,4},{4,8},{8,12},{12,0},{1,5},{5,9},{9,13},{13,1},{2,6},{6,10},{... | collective-permute-start | bytes 589832 | tf_op jit(solution)/shard_map/ppermute | solution.py:505
  9.5 4.2 %collective-permute-done.3.refs_2_ = bf16[96,1024]{1,0:T(8,128)(2,1)S(1)} collective-permute-done((bf16[96,1024]{1,0:T(8,128)(2,1)S(1)}, bf16[96,1024]{1,0:T(8,128)(2,1)S(1)}, u32[]{:S(2)}, u32[]{:S(2)}) %collective-permute-start.3) | collective-permute-done | bytes 196640 | tf_op jit(solution)/shard_map/ppermute | solution.py:504
  13.7 3.9 %collective-permute-done.refs_5_ = bf16[384,256]{1,0:T(8,128)(2,1)S(1)} collective-permute-done((bf16[384,256]{1,0:T(8,128)(2,1)S(1)}, bf16[384,256]{1,0:T(8,128)(2,1)S(1)}, u32[]{:S(2)}, u32[]{:S(2)}) %collective-permute-start) | collective-permute-done | bytes 196640 | tf_op jit(solution)/shard_map/ppermute | solution.py:505
  17.6 0.0 collective-permute-start.1
  17.6 4.2 %collective-permute-done.4.refs_3_ = bf16[96,1024]{1,0:T(8,128)(2,1)S(1)} collective-permute-done((bf16[96,1024]{1,0:T(8,128)(2,1)S(1)}, bf16[96,1024]{1,0:T(8,128)(2,1)S(1)}, u32[]{:S(2)}, u32[]{:S(2)}) %collective-permute-start.4) | collective-permute-done | bytes 196640 | tf_op jit(solution)/shard_map/ppermute | solution.py:504
  21.9 5.3 %collective-permute-done.1.refs_6_ = bf16[384,256]{1,0:T(8,128)(2,1)S(1)} collective-permute-done((bf16[384,256]{1,0:T(8,128)(2,1)S(1)}, bf16[384,256]{1,0:T(8,128)(2,1)S(1)}, u32[]{:S(2)}, u32[]{:S(2)}) %collective-permute-start.1) | collective-permute-done | bytes 196640 | tf_op jit(solution)/shard_map/ppermute | solution.py:505
  27.2 1.2 %copy-done.1 = bf16[8,128,512]{2,1,0:T(8,128)(2,1)S(1)} copy-done((bf16[8,128,512]{2,1,0:T(8,128)(2,1)S(1)}, bf16[8,128,512]{2,1,0:T(8,128)(2,1)}, u32[]{:S(2)}) %copy-start.1) | copy-done | bytes 1048600
  28.4 1.0 %copy-done.2 = bf16[4,32,2048]{2,1,0:T(8,128)(2,1)S(1)} copy-done((bf16[4,32,2048]{2,1,0:T(8,128)(2,1)S(1)}, bf16[4,32,2048]{2,1,0:T(8,128)(2,1)}, u32[]{:S(2)}) %copy-start.2) | copy-done | bytes 524312
  29.5 0.8 %copy-done.8 = bf16[8,4,512]{2,1,0:T(4,128)(2,1)S(1)} copy-done((bf16[8,4,512]{2,1,0:T(4,128)(2,1)S(1)}, bf16[8,4,512]{2,1,0:T(4,128)(2,1)}, u32[]{:S(2)}) %copy-start.8) | copy-done | bytes 32792
  30.2 0.8 %copy-done.9 = bf16[8,4,512]{2,1,0:T(4,128)(2,1)S(1)} copy-done((bf16[8,4,512]{2,1,0:T(4,128)(2,1)S(1)}, bf16[8,4,512]{2,1,0:T(4,128)(2,1)}, u32[]{:S(2)}) %copy-start.9) | copy-done | bytes 32792
  31.0 0.7 %copy-done.10 = s32[4]{0:T(128)S(1)} copy-done((s32[4]{0:T(128)S(1)}, s32[4]{0:T(128)}, u32[]{:S(2)}) %copy-start.10) | copy-done | bytes 40
  31.6 0.7 %copy-done.11 = s32[8]{0:T(128)S(1)} copy-done((s32[8]{0:T(128)S(1)}, s32[8]{0:T(128)}, u32[]{:S(2)}) %copy-start.11) | copy-done | bytes 56
  32.3 0.7 %copy-done.12 = s32[8]{0:T(128)S(1)} copy-done((s32[8]{0:T(128)S(1)}, s32[8]{0:T(128)}, u32[]{:S(2)}) %copy-start.12) | copy-done | bytes 56
  33.0 3.0 %prepare.1 = (f32[2,80,128]{2,1,0:T(8,128)S(1)}, bf16[4,2,256,128]{3,2,1,0:T(8,128)(2,1)S(1)}, bf16[2,256,512]{2,1,0:T(8,128)(2,1)S(1)}, f32[2,128,256]{2,1,0:T(8,128)S(1)}, f32[2,8,256]{2,1,0:T(8,128)S(1)}) custom-call(s32[4]{0:T(128)S(1)} %copy-done.10, s32[8]{0:T(128)S(1)} %copy-done.11, s32[8]{0:T(128)S(1)} %copy-done.12, ...), custom_call_target="tpu_custom_call" | custom-call | tf_op jit(solution)/shard_map/prepare/pallas_call | solution.py:508
  36.0 3.9 %near.1 = (f32[4,2,128,256]{3,2,1,0:T(8,128)S(1)}, f32[4,2,8,256]{3,2,1,0:T(8,128)S(1)}, f32[2,128,256]{2,1,0:T(8,128)S(1)}, f32[2,8,256]{2,1,0:T(8,128)S(1)}) custom-call(s32[4]{0:T(128)S(1)} %copy-done.10, bf16[96,1024]{1,0:T(8,128)(2,1)S(1)} %pack_keys.1.refs_1_, bf16[96,1024]{1,0:T(8,128)(2,1)S(1)} %collective-permute-done.3.refs_2_, ...), custom_call_target="tpu_custom_call" | custom-call | tf_op jit(solution)/shard_map/near/pallas_call | solution.py:547
  39.9 1.6 %far.1 = (f32[4,2,256,128]{3,2,1,0:T(8,128)S(1)}, bf16[4,2,256,96]{3,2,1,0:T(8,128)(2,1)S(1)}, f32[2,256,128]{2,1,0:T(8,128)S(1)}, bf16[2,256,384]{2,1,0:T(8,128)(2,1)S(1)}) custom-call(s32[4]{0:T(128)S(1)} %copy-done.10, bf16[96,1024]{1,0:T(8,128)(2,1)S(1)} %collective-permute-done.5.key_ref, f32[2,80,128]{2,1,0:T(8,128)S(1)} %get-tuple-element.15.refs_7_.table_ref, ...), custom_call_target="tpu_custom_call" | custom-call | tf_op jit(solution)/shard_map/far/pallas_call | solution.py:557
  41.6 1.1 %last.1 = (bf16[4,32,2048]{2,1,0:T(8,128)(2,1)}, bf16[8,4,2048]{2,1,0:T(4,128)(2,1)}) custom-call(bf16[384,256]{1,0:T(8,128)(2,1)S(1)} %collective-permute-done.2.value_ref, f32[4,2,256,128]{3,2,1,0:T(8,128)S(1)} %get-tuple-element.24.base_ref, bf16[4,2,256,96]{3,2,1,0:T(8,128)(2,1)S(1)} %get-tuple-element.25.weight_ref, ...), custom_call_target="tpu_custom_call" | custom-call | tf_op jit(solution)/shard_map/last/pallas_call | solution.py:573
  (20 shorter events, 0.1 us)
Async XLA Ops:
  0.6 26.6 %copy-start = (bf16[8,128,512]{2,1,0:T(8,128)(2,1)S(1)}, bf16[8,128,512]{2,1,0:T(8,128)(2,1)}, u32[]{:S(2)}) copy-start(bf16[8,128,512]{2,1,0:T(8,128)(2,1)} %gen_k_ref.1) | copy-start | bytes 3145732
  0.6 1.0 %copy-start.3 = (bf16[4,64,512]{2,1,0:T(8,128)(2,1)S(1)}, bf16[4,64,512]{2,1,0:T(8,128)(2,1)}, u32[]{:S(2)}) copy-start(bf16[4,64,512]{2,1,0:T(8,128)(2,1)} %cache_ref.3) | copy-start | bytes 786436
  1.7 0.9 %copy-start.6 = (bf16[4,32,512]{2,1,0:T(8,128)(2,1)S(1)}, bf16[4,32,512]{2,1,0:T(8,128)(2,1)}, u32[]{:S(2)}) copy-start(bf16[4,32,512]{2,1,0:T(8,128)(2,1)} %span_ref.3) | copy-start | bytes 393220
  2.8 10.9 %collective-permute-start.3 = (bf16[96,1024]{1,0:T(8,128)(2,1)S(1)}, bf16[96,1024]{1,0:T(8,128)(2,1)S(1)}, u32[]{:S(2)}, u32[]{:S(2)}) collective-permute-start(bf16[96,1024]{1,0:T(8,128)(2,1)S(1)} %pack_keys.1.refs_1_), channel_id=1, source_target_pairs={{0,4},{4,8},{8,12},{12,0},{1,5},{5,9},{9,13},{13,1},{2,6},{6,10},{... | collective-permute-start | bytes 589832 | tf_op jit(solution)/shard_map/ppermute | solution.py:504
  5.9 0.9 %copy-start.4 = (bf16[4,64,512]{2,1,0:T(8,128)(2,1)S(1)}, bf16[4,64,512]{2,1,0:T(8,128)(2,1)}, u32[]{:S(2)}) copy-start(bf16[4,64,512]{2,1,0:T(8,128)(2,1)} %cache_ref.2) | copy-start | bytes 786436
  6.9 0.9 %copy-start.7 = (bf16[4,32,512]{2,1,0:T(8,128)(2,1)S(1)}, bf16[4,32,512]{2,1,0:T(8,128)(2,1)}, u32[]{:S(2)}) copy-start(bf16[4,32,512]{2,1,0:T(8,128)(2,1)} %span_ref.2) | copy-start | bytes 393220
  7.8 19.4 %copy-start.5 = (bf16[8,4,2048]{2,1,0:T(4,128)(2,1)S(1)}, bf16[8,4,2048]{2,1,0:T(4,128)(2,1)}, u32[]{:S(2)}) copy-start(bf16[8,4,2048]{2,1,0:T(4,128)(2,1)} %dec_q_ref.1) | copy-start | bytes 393220
  7.9 9.7 %collective-permute-start = (bf16[384,256]{1,0:T(8,128)(2,1)S(1)}, bf16[384,256]{1,0:T(8,128)(2,1)S(1)}, u32[]{:S(2)}, u32[]{:S(2)}) collective-permute-start(bf16[384,256]{1,0:T(8,128)(2,1)S(1)} %pack_values.1.refs_4_), channel_id=1, source_target_pairs={{0,4},{4,8},{8,12},{12,0},{1,5},{5,9},{9,13},{13,1},{2,6},{6,10},{... | collective-permute-start | bytes 589832 | tf_op jit(solution)/shard_map/ppermute | solution.py:505
  13.7 8.1 %collective-permute-start.4 = (bf16[96,1024]{1,0:T(8,128)(2,1)S(1)}, bf16[96,1024]{1,0:T(8,128)(2,1)S(1)}, u32[]{:S(2)}, u32[]{:S(2)}) collective-permute-start(bf16[96,1024]{1,0:T(8,128)(2,1)S(1)} %collective-permute-done.3.refs_2_), channel_id=1, source_target_pairs={{0,4},{4,8},{8,12},{12,0},{1,5},{5,9},{9,13},{13,1},{2,6},{6,10},{... | collective-permute-start | bytes 589832 | tf_op jit(solution)/shard_map/ppermute | solution.py:504
  17.6 9.6 %collective-permute-start.1 = (bf16[384,256]{1,0:T(8,128)(2,1)S(1)}, bf16[384,256]{1,0:T(8,128)(2,1)S(1)}, u32[]{:S(2)}, u32[]{:S(2)}) collective-permute-start(bf16[384,256]{1,0:T(8,128)(2,1)S(1)} %collective-permute-done.refs_5_), channel_id=1, source_target_pairs={{0,4},{4,8},{8,12},{12,0},{1,5},{5,9},{9,13},{13,1},{2,6},{6,10},{... | collective-permute-start | bytes 589832 | tf_op jit(solution)/shard_map/ppermute | solution.py:505
  21.8 18.1 %collective-permute-start.5 = (bf16[96,1024]{1,0:T(8,128)(2,1)S(1)}, bf16[96,1024]{1,0:T(8,128)(2,1)S(1)}, u32[]{:S(2)}, u32[]{:S(2)}) collective-permute-start(bf16[96,1024]{1,0:T(8,128)(2,1)S(1)} %collective-permute-done.4.refs_3_), channel_id=1, source_target_pairs={{0,4},{4,8},{8,12},{12,0},{1,5},{5,9},{9,13},{13,1},{2,6},{6,10},{... | collective-permute-start | bytes 589832 | tf_op jit(solution)/shard_map/ppermute | solution.py:504
  27.2 14.4 %collective-permute-start.2 = (bf16[384,256]{1,0:T(8,128)(2,1)S(1)}, bf16[384,256]{1,0:T(8,128)(2,1)S(1)}, u32[]{:S(2)}, u32[]{:S(2)}) collective-permute-start(bf16[384,256]{1,0:T(8,128)(2,1)S(1)} %collective-permute-done.1.refs_6_), channel_id=1, source_target_pairs={{0,4},{4,8},{8,12},{12,0},{1,5},{5,9},{9,13},{13,1},{2,6},{6,10},{... | collective-permute-start | bytes 589832 | tf_op jit(solution)/shard_map/ppermute | solution.py:505
  27.2 1.2 %copy-start.1 = (bf16[8,128,512]{2,1,0:T(8,128)(2,1)S(1)}, bf16[8,128,512]{2,1,0:T(8,128)(2,1)}, u32[]{:S(2)}) copy-start(bf16[8,128,512]{2,1,0:T(8,128)(2,1)} %gen_v_ref.1) | copy-start | bytes 3145732
  28.4 1.0 %copy-start.2 = (bf16[4,32,2048]{2,1,0:T(8,128)(2,1)S(1)}, bf16[4,32,2048]{2,1,0:T(8,128)(2,1)}, u32[]{:S(2)}) copy-start(bf16[4,32,2048]{2,1,0:T(8,128)(2,1)} %span_q_ref.1) | copy-start | bytes 1572868
  29.5 0.8 %copy-start.8 = (bf16[8,4,512]{2,1,0:T(4,128)(2,1)S(1)}, bf16[8,4,512]{2,1,0:T(4,128)(2,1)}, u32[]{:S(2)}) copy-start(bf16[8,4,512]{2,1,0:T(4,128)(2,1)} %new_k_ref.1) | copy-start | bytes 98308
  30.2 0.8 %copy-start.9 = (bf16[8,4,512]{2,1,0:T(4,128)(2,1)S(1)}, bf16[8,4,512]{2,1,0:T(4,128)(2,1)}, u32[]{:S(2)}) copy-start(bf16[8,4,512]{2,1,0:T(4,128)(2,1)} %new_v_ref.1) | copy-start | bytes 98308
  31.0 0.7 %copy-start.10 = (s32[4]{0:T(128)S(1)}, s32[4]{0:T(128)}, u32[]{:S(2)}) copy-start(s32[4]{0:T(128)} %begin_ref.3) | copy-start | bytes 52
  31.6 0.7 %copy-start.11 = (s32[8]{0:T(128)S(1)}, s32[8]{0:T(128)}, u32[]{:S(2)}) copy-start(s32[8]{0:T(128)} %request_ref.1) | copy-start | bytes 100
  32.3 0.7 %copy-start.12 = (s32[8]{0:T(128)S(1)}, s32[8]{0:T(128)}, u32[]{:S(2)}) copy-start(s32[8]{0:T(128)} %length_ref.1) | copy-start | bytes 100
where the time goes:
time: 43.1 us; the launch traced here: 42.7 us
  waiting for transfers between devices  17.6 us (41%)
  Pallas kernels  10 us (23%)
  local copies, waits for them, and re-layouts  9.54 us (22%)
  starting transfers between devices  4.81 us (11%)
  between operations  0.72 us (2%)
    unnamed x26, local copies, waits for them, and re-layouts  9.54 us
    ppermute x3, waiting for transfers between devices, body(): values.append(lax.ppermute(values[-1], 'seq', ring))  9.25 us
    ppermute x3, waiting for transfers between devices, body(): keys.append(lax.ppermute(keys[-1], 'seq', ring))  8.35 us
    pallas_call x1, Pallas kernels, body(): pl.pallas_call(functools.partial(near_kernel, shards, used, ch, count), o...  3.91 us
    ppermute x3, starting transfers between devices, body(): keys.append(lax.ppermute(keys[-1], 'seq', ring))  3.14 us
    pallas_call x1, Pallas kernels, body(): pl.pallas_call(functools.partial(prepare_kernel, shards, q_heads, kv_loca...  3.02 us
    ppermute x3, starting transfers between devices, body(): values.append(lax.ppermute(values[-1], 'seq', ring))  1.66 us
    pallas_call x1, Pallas kernels, body(): pl.pallas_call(functools.partial(far_kernel, shards, used, ch), out_shape...  1.65 us
  transfers between devices with their start and end apart: 6, of which 4 were waited for; matrix products, arithmetic and copies ran while one was open for 0% of the time, Pallas kernels for 20%

commit v1 on v0

--- a/solution.py
+++ b/solution.py
@@ -8,6 +8,7 @@
 from jax.experimental.pallas import tpu as pltpu
 from jax.sharding import PartitionSpec as P
 
+
 QUERY_HEADS = 64
 KEY_VALUE_HEADS = 8
 HEAD_WIDTH = 128
@@ -16,11 +17,22 @@
 
 very_low = -1e30
 RATE = HEAD_WIDTH ** (-0.5) * math.log2(math.e)
+ANY = pl.BlockSpec(memory_space=pl.ANY)
 HBM = pl.BlockSpec(memory_space=pltpu.HBM)
 SMEM = pl.BlockSpec(memory_space=pltpu.SMEM)
 VMEM = pl.BlockSpec(memory_space=pltpu.VMEM)
 bf16 = jnp.bfloat16
 f32 = jnp.float32
+
+
+def in_hbm(*arrays):
+    return [pltpu.with_memory_space_constraint(array, pltpu.HBM) for array in arrays]
+
+
+def cost(micros):
+    return pl.CostEstimate(
+        flops=int(micros * 1e9), bytes_accessed=int(micros * 3e6), transcendentals=0
+    )
 
 
 def tile(n):
@@ -96,7 +108,8 @@
         copy.wait()
 
 
-def pack_values_kernel(q_heads, kv_local, used, cache_ref, span_ref, out_ref, sem):
+def pack_values_kernel(q_heads, kv_local, used, cache_ref, span_ref, after_ref, out_ref, sem):
+    del after_ref
     prompts, pre, _ = cache_ref.shape
     ch = span_ref.shape[1]
     first = first_head(q_heads, kv_local)
@@ -137,6 +150,10 @@
     q_cat_ref,
     acc_ref,
     stat_ref,
+    sq_scr,
+    dq_scr,
+    nk_scr,
+    nv_scr,
     gk_scr,
     gv_scr,
     q_scr,
@@ -151,8 +168,12 @@
     first = first_head(q_heads, kv_local)
     lanes = pl.ds(pl.multiple_of(first * HEAD_WIDTH, HEAD_WIDTH), used * HEAD_WIDTH)
     copies = [
-        pltpu.make_async_copy(src.at[:, :, lanes], dst, sem.at[i])
-        for i, (src, dst) in enumerate(((gen_k_ref, gk_scr), (gen_v_ref, gv_scr)))
+        pltpu.make_async_copy(span_q_ref, sq_scr, sem.at[0]),
+        pltpu.make_async_copy(dec_q_ref, dq_scr, sem.at[1]),
+        pltpu.make_async_copy(new_k_ref.at[:, :, lanes], nk_scr, sem.at[2]),
+        pltpu.make_async_copy(new_v_ref.at[:, :, lanes], nv_scr, sem.at[3]),
+        pltpu.make_async_copy(gen_k_ref.at[:, :, lanes], gk_scr, sem.at[4]),
+        pltpu.make_async_copy(gen_v_ref.at[:, :, lanes], gv_scr, sem.at[5]),
     ]
     for copy in copies:
         copy.start()
@@ -176,13 +197,16 @@
     table_ref[0] = cosine
     table_ref[1] = sine
 
+    copies[0].wait()
     for p in range(prompts):
         cosine, sine = token_tables(table_ref, ch, ch + p * shards + me)
         for h in range(used):
             for g in range(per_kv):
-                x = span_q_ref[p, :, tile(h * per_kv + g)].astype(f32)
+                x = sq_scr[p, :, tile(h * per_kv + g)].astype(f32)
                 q_ref[p, h, pl.ds(g * ch, ch), :] = rotate(x, cosine, sine).astype(bf16)
 
+    for copy in copies[1:4]:
+        copy.wait()
     n_scr[...] = jnp.zeros_like(n_scr)
     pad = n_scr.shape[2]
     for r in range(rows_local):
@@ -191,13 +215,12 @@
         sine = signed(table_ref[1, rows, :])
         for h in range(used):
             for g in range(per_kv):
-                x = dec_q_ref[r, :, tile(h * per_kv + g)].astype(f32)
+                x = dq_scr[r, :, tile(h * per_kv + g)].astype(f32)
                 q_scr[h, pl.ds(r * step_rows + g * steps, steps), :] = rotate(x, cosine, sine)
-            own = pl.ds(pl.multiple_of((first + h) * HEAD_WIDTH, HEAD_WIDTH), HEAD_WIDTH)
             n_scr[0, r * used + h, pl.ds(0, steps), :] = rotate(
-                new_k_ref[r, :, own].astype(f32), cosine, sine
+                nk_scr[r, :, tile(h)].astype(f32), cosine, sine
             )
-            n_scr[1, r * used + h, pl.ds(0, steps), :] = new_v_ref[r, :, own].astype(f32)
+            n_scr[1, r * used + h, pl.ds(0, steps), :] = nv_scr[r, :, tile(h)].astype(f32)
 
     for h in range(used):
         for r in range(rows_local):
@@ -206,7 +229,7 @@
             for p in range(prompts):
                 q_cat_ref[h, rows, tile(p)] = jnp.where(request_ref[r] == p, x, 0.0).astype(bf16)
 
-    for copy in copies:
+    for copy in copies[4:]:
         copy.wait()
     span = min(HEAD_WIDTH, dec_rows)
     group = span // step_rows
@@ -262,7 +285,6 @@
 
 
 def hide(scores, pre, begin, last):
-    n, lanes = scores.shape
     low = scores[:pre]
     low = jnp.where(iota(low.shape, 0) < begin, low, very_low)
     high = scores[pre:]
@@ -277,17 +299,18 @@
     )
 
 
-def near_kernel(shards, used, ch, count, *refs):
+def near_kernel(shards, used, ch, hops, *refs):
+    count = len(hops)
     begin_ref = refs[0]
     keys, values = refs[1 : 1 + count], refs[1 + count : 1 + 2 * count]
     table_ref, q_ref, q_cat_ref, acc_in_ref, stat_in_ref = refs[1 + 2 * count : 6 + 2 * count]
-    acc_ref, stat_ref, dec_acc_ref, dec_stat_ref, k_scr = refs[6 + 2 * count :]
+    before = refs[6 + 2 * count : -5]
+    acc_ref, stat_ref, dec_acc_ref, dec_stat_ref, k_scr = refs[-5:]
     prompts, _, rows, _ = q_ref.shape
     size = keys[0].shape[0]
-    dec_rows = q_cat_ref.shape[1]
     me = lax.axis_index("seq")
     pre = size - ch
-    shard = [lax.rem(me + shards - c, shards) for c in range(count)]
+    shard = [lax.rem(me + shards - hop, shards) for hop in hops]
     for c in range(count):
         rotate_keys(
             keys[c], k_scr, table_ref, shards, prompts, used, pre, ch, shard[c], c * size
@@ -310,12 +333,20 @@
                 )
             scores = jnp.concatenate(pieces, axis=0)
             top = jnp.max(scores, axis=0, keepdims=True)
+            if before:
+                old_top = before[1][p, h, pl.ds(0, 1), :]
+                top = jnp.maximum(top, old_top)
             weights = jnp.exp2((scores - top) * RATE)
             total = jnp.sum(weights, axis=0, keepdims=True)
             v = jnp.concatenate(
                 [ref[pl.ds(p * size, size), tile(h)] for ref in values], axis=0
             )
-            acc_ref[p, h] = dot_tn(v, weights.astype(bf16))
+            acc = dot_tn(v, weights.astype(bf16))
+            if before:
+                factor = jnp.exp2((old_top - top) * RATE)
+                total = total + before[1][p, h, pl.ds(1, 1), :] * factor
+                acc = acc + before[0][p, h] * factor
+            acc_ref[p, h] = acc
             stat_ref[p, h, pl.ds(0, 1), :] = top
             stat_ref[p, h, pl.ds(1, 1), :] = total
 
@@ -485,22 +516,24 @@
         out_specs=VMEM,
         scratch_shapes=[pltpu.SemaphoreType.DMA((prompts, used, 2))],
         compiler_params=params(),
+        cost_estimate=cost(1),
         name="pack_keys",
-    )(prompt_cache_keys, span_raw_keys)
+    )(*in_hbm(prompt_cache_keys, span_raw_keys))
     own_values = pl.pallas_call(
         functools.partial(pack_values_kernel, q_heads, kv_local, used),
         out_shape=shape((prompts * size, width), bf16),
-        in_specs=[HBM, HBM],
+        in_specs=[HBM, HBM, ANY],
         out_specs=VMEM,
         scratch_shapes=[pltpu.SemaphoreType.DMA((prompts, 2))],
         compiler_params=params(),
+        cost_estimate=cost(1),
         name="pack_values",
-    )(prompt_cache_values, span_raw_values)
+    )(*in_hbm(prompt_cache_values, span_raw_values), own_keys)
 
     ring = [(i, (i + 1) % shards) for i in range(shards)]
     keys = [own_keys]
     values = [own_values]
-    for _ in range(shards - 1):
+    for _ in range(1, shards):
         keys.append(lax.ppermute(keys[-1], "seq", ring))
         values.append(lax.ppermute(values[-1], "seq", ring))
 
@@ -514,45 +547,55 @@
             shape((used, HEAD_WIDTH, dec_rows), f32),
             shape((used, 8, dec_rows), f32),
         ],
-        in_specs=[SMEM] * 3 + [VMEM] * 4 + [HBM] * 2,
+        in_specs=[SMEM] * 3 + [HBM] * 6,
         out_specs=[VMEM] * 5,
         scratch_shapes=[
+            pltpu.VMEM(span_q.shape, bf16),
+            pltpu.VMEM(decode_new_queries.shape, bf16),
+            pltpu.VMEM((rows_local, steps, width), bf16),
+            pltpu.VMEM((rows_local, steps, width), bf16),
             pltpu.VMEM((rows_local, gen, width), bf16),
             pltpu.VMEM((rows_local, gen, width), bf16),
             pltpu.VMEM((used, dec_rows, HEAD_WIDTH), f32),
             pltpu.VMEM((2, rows_local * used, 16, HEAD_WIDTH), f32),
-            pltpu.SemaphoreType.DMA((2,)),
+            pltpu.SemaphoreType.DMA((6,)),
         ],
         compiler_params=params(),
+        cost_estimate=cost(3),
         name="prepare",
     )(
         span_offsets,
         row_request,
         row_length,
-        span_q,
-        decode_new_queries,
-        decode_new_keys,
-        decode_new_values,
-        generated_keys,
-        generated_values,
+        *in_hbm(
+            span_q,
+            decode_new_queries,
+            decode_new_keys,
+            decode_new_values,
+            generated_keys,
+            generated_values,
+        ),
     )
 
-    count = shards - 1
-    state = [
+    prompt_state = [
         shape((prompts, used, HEAD_WIDTH, rows), f32),
         shape((prompts, used, 8, rows), f32),
-        shape((used, HEAD_WIDTH, dec_rows), f32),
-        shape((used, 8, dec_rows), f32),
     ]
-    near = pl.pallas_call(
-        functools.partial(near_kernel, shards, used, ch, count),
-        out_shape=state,
-        in_specs=[SMEM] + [VMEM] * (2 * count + 5),
-        out_specs=[VMEM] * 4,
-        scratch_shapes=[pltpu.VMEM((count * size, prompts * width), bf16)],
-        compiler_params=params(),
-        name="near",
-    )(span_offsets, *keys[:-1], *values[:-1], table, queries, dec_queries, gen_acc, gen_stat)
+    row_state = [shape((used, HEAD_WIDTH, dec_rows), f32), shape((used, 8, dec_rows), f32)]
+    near = [gen_acc, gen_stat]
+    for step in range(1, max(2, shards - 1)):
+        hops = [hop for hop in ([0, 1] if step == 1 else [step]) if hop < shards - 1]
+        ins = [span_offsets, *[keys[hop] for hop in hops], *[values[hop] for hop in hops]]
+        ins += [table, queries, dec_queries, *near[-2:], *near[:-2]]
+        near = pl.pallas_call(
+            functools.partial(near_kernel, shards, used, ch, hops),
+            out_shape=prompt_state + row_state,
+            in_specs=[SMEM] + [VMEM] * (len(ins) - 1),
+            out_specs=[VMEM] * 4,
+            scratch_shapes=[pltpu.VMEM((len(hops) * size, prompts * width), bf16)],
+            compiler_params=params(),
+            cost_estimate=cost(3),
+        )(*ins)
 
     far = pl.pallas_call(
         functools.partial(far_kernel, shards, used, ch),
@@ -566,6 +609,7 @@
         out_specs=[VMEM] * 4,
         scratch_shapes=[pltpu.VMEM((size, prompts * width), bf16)],
         compiler_params=params(),
+        cost_estimate=cost(2),
         name="far",
     )(span_offsets, keys[-1], table, queries, dec_queries, *near)
 
@@ -584,7 +628,8 @@
                 pltpu.SemaphoreType.DMA((prompts + 1,)),
             ],
             compiler_params=params(),
-            name="last",
+            cost_estimate=cost(1),
+        name="last",
         )(values[-1], *far)
     )
 

time: 43.1 us -> 40.2 us (0.933)
  local copies, waits for them, and re-layouts: 9.54 us -> 0.02 us
  Pallas kernels: 10 us -> 13.6 us
  waiting for transfers between devices: 17.6 us -> 19.5 us
  starting transfers between devices: 4.81 us -> 6.03 us
    unnamed x26 -> x6, local copies, waits for them, and re-layouts: 9.54 us -> 0.02 us
    ppermute x3, waiting for transfers between devices: 8.35 us -> 9.73 us  [body(): keys.append(lax.ppermute(keys[-1], 'seq', ring))]
    ppermute x3, starting transfers between devices: 3.14 us -> 4.4 us  [body(): keys.append(lax.ppermute(keys[-1], 'seq', ring))]
    pallas_call x1 -> x2, Pallas kernels: 3.91 us -> 5.11 us  [body(): pl.pallas_call(functools.partial(near_kernel, shards, used, ch, hops), ou...]
    pallas_call x1, Pallas kernels: 0.22 us -> 1.05 us  [body(): pl.pallas_call(functools.partial(pack_keys_kernel, q_heads, kv_local, use...]
    pallas_call x1, Pallas kernels: 0.12 us -> 0.93 us  [body(): pl.pallas_call(functools.partial(pack_values_kernel, q_heads, kv_local, u...]
    pallas_call x1, Pallas kernels: 3.02 us -> 3.8 us  [body(): pl.pallas_call(functools.partial(prepare_kernel, shards, q_heads, kv_loca...]
    ppermute x3, waiting for transfers between devices: 9.25 us -> 9.81 us  [body(): values.append(lax.ppermute(values[-1], 'seq', ring))]
  transfers between devices with their start and end apart: 6 -> 6, of which waited for: 4 -> 4; matrix products, arithmetic and copies ran while one was open for 0% -> 0% of each run, Pallas kernels for 20% -> 29%
where the time goes in v1:
time: 40.2 us; the launch traced here: 39.9 us
  waiting for transfers between devices  19.5 us (49%)
  Pallas kernels  13.6 us (34%)
  starting transfers between devices  6.03 us (15%)
  between operations  0.71 us (2%)
    ppermute x3, waiting for transfers between devices, body(): values.append(lax.ppermute(values[-1], 'seq', ring))  9.81 us
    ppermute x3, waiting for transfers between devices, body(): keys.append(lax.ppermute(keys[-1], 'seq', ring))  9.73 us
    pallas_call x2, Pallas kernels, body(): pl.pallas_call(functools.partial(near_kernel, shards, used, ch, hops), ou...  5.11 us
    ppermute x3, starting transfers between devices, body(): keys.append(lax.ppermute(keys[-1], 'seq', ring))  4.4 us
    pallas_call x1, Pallas kernels, body(): pl.pallas_call(functools.partial(prepare_kernel, shards, q_heads, kv_loca...  3.8 us
    ppermute x3, starting transfers between devices, body(): values.append(lax.ppermute(values[-1], 'seq', ring))  1.63 us
    pallas_call x1, Pallas kernels, body(): pl.pallas_call(functools.partial(far_kernel, shards, used, ch), out_shape...  1.63 us
    pallas_call x1, Pallas kernels, body(): pl.pallas_call(functools.partial(last_kernel, used, per_kv, steps), out_s...  1.09 us
  transfers between devices with their start and end apart: 6, of which 4 were waited for; matrix products, arithmetic and copies ran while one was open for 0% of the time, Pallas kernels for 29%

profile of v1, /device:TPU:0, one launch (start us, length us, event | category | flops | bytes accessed | tf_op | source)
XLA Modules:
  0.0 39.9 jit_solution(12219191914298446431)
XLA Ops:
  0.6 1.0 %pack_keys.1.after_ref.refs_1_ = bf16[96,1024]{1,0:T(8,128)(2,1)S(1)} custom-call(bf16[4,64,512]{2,1,0:T(8,128)(2,1)} %cache_ref.2, bf16[4,32,512]{2,1,0:T(8,128)(2,1)} %span_ref.2), custom_call_target="tpu_custom_call" | custom-call | flops 1000000000 | bytes 3000000 | tf_op jit(solution)/shard_map/pack_keys/pallas_call | solution.py:512
  1.7 0.0 copy-start
  1.7 0.0 copy-start.1
  1.7 0.0 copy-start.2
  1.7 3.1 %collective-permute-start.3 = (bf16[96,1024]{1,0:T(8,128)(2,1)S(1)}, bf16[96,1024]{1,0:T(8,128)(2,1)S(1)}, u32[]{:S(2)}, u32[]{:S(2)}) collective-permute-start(bf16[96,1024]{1,0:T(8,128)(2,1)S(1)} %pack_keys.1.after_ref.refs_1_), channel_id=1, source_target_pairs={{0,4},{4,8},{8,12},{12,0},{1,5},{5,9},{9,13},{13,1},{2,6},{6,10},{... | collective-permute-start | bytes 589832 | tf_op jit(solution)/shard_map/ppermute | solution.py:537
  4.8 0.9 %pack_values.1.refs_3_ = bf16[384,256]{1,0:T(8,128)(2,1)S(1)} custom-call(bf16[4,64,512]{2,1,0:T(8,128)(2,1)} %cache_ref.3, bf16[4,32,512]{2,1,0:T(8,128)(2,1)} %span_ref.3, bf16[96,1024]{1,0:T(8,128)(2,1)S(1)} %pack_keys.1.after_ref.refs_1_), custom_call_target="tpu_custom_call" | custom-call | flops 1000000000 | bytes 3000000 | tf_op jit(solution)/shard_map/pack_values/pallas_call | solution.py:522
  5.8 1.6 %collective-permute-start = (bf16[384,256]{1,0:T(8,128)(2,1)S(1)}, bf16[384,256]{1,0:T(8,128)(2,1)S(1)}, u32[]{:S(2)}, u32[]{:S(2)}) collective-permute-start(bf16[384,256]{1,0:T(8,128)(2,1)S(1)} %pack_values.1.refs_3_), channel_id=1, source_target_pairs={{0,4},{4,8},{8,12},{12,0},{1,5},{5,9},{9,13},{13,1},{2,6},{6,10},{... | collective-permute-start | bytes 589832 | tf_op jit(solution)/shard_map/ppermute | solution.py:538
  7.4 0.0 copy-done
  7.4 0.0 copy-done.1
  7.4 3.8 %prepare.1 = (f32[2,80,128]{2,1,0:T(8,128)S(1)}, bf16[4,2,256,128]{3,2,1,0:T(8,128)(2,1)S(1)}, bf16[2,256,512]{2,1,0:T(8,128)(2,1)S(1)}, f32[2,128,256]{2,1,0:T(8,128)S(1)}, f32[2,8,256]{2,1,0:T(8,128)S(1)}) custom-call(s32[4]{0:T(128)S(1)} %copy-done.2, s32[8]{0:T(128)S(1)} %copy-done, s32[8]{0:T(128)S(1)} %copy-done.1, bf16[4,32,2048]{2,1,0:T(8,128)(2,1)} %span_q_ref.1, ...), custom_call_target="tpu_custom_call" | custom-call | flops 3000000000 | bytes 9000000 | tf_op jit(solution)/shard_map/prepare/pallas_call | solution.py:541
  11.2 4.8 %collective-permute-done.refs_4_ = bf16[384,256]{1,0:T(8,128)(2,1)S(1)} collective-permute-done((bf16[384,256]{1,0:T(8,128)(2,1)S(1)}, bf16[384,256]{1,0:T(8,128)(2,1)S(1)}, u32[]{:S(2)}, u32[]{:S(2)}) %collective-permute-start) | collective-permute-done | bytes 196640 | tf_op jit(solution)/shard_map/ppermute | solution.py:538
  16.0 0.0 collective-permute-start.1
  16.0 0.0 collective-permute-done.3.refs_2_
  16.0 1.3 %collective-permute-start.4 = (bf16[96,1024]{1,0:T(8,128)(2,1)S(1)}, bf16[96,1024]{1,0:T(8,128)(2,1)S(1)}, u32[]{:S(2)}, u32[]{:S(2)}) collective-permute-start(bf16[96,1024]{1,0:T(8,128)(2,1)S(1)} %collective-permute-done.3.refs_2_), channel_id=1, source_target_pairs={{0,4},{4,8},{8,12},{12,0},{1,5},{5,9},{9,13},{13,1},{2,6},{6,10},{... | collective-permute-start | bytes 589832 | tf_op jit(solution)/shard_map/ppermute | solution.py:537
  17.3 3.2 %shard_map.140 = (f32[4,2,128,256]{3,2,1,0:T(8,128)S(1)}, f32[4,2,8,256]{3,2,1,0:T(8,128)S(1)}, f32[2,128,256]{2,1,0:T(8,128)S(1)}, f32[2,8,256]{2,1,0:T(8,128)S(1)}) custom-call(s32[4]{0:T(128)S(1)} %copy-done.2, bf16[96,1024]{1,0:T(8,128)(2,1)S(1)} %pack_keys.1.after_ref.refs_1_, bf16[96,1024]{1,0:T(8,128)(2,1)S(1)} %collective-permute-done.3.refs_2_, ...), custom_call_target="tpu_custom_call" | custom-call | flops 3000000000 | bytes 9000000 | tf_op jit(solution)/shard_map/pallas_call | solution.py:590
  20.5 5.0 %collective-permute-done.1.refs_2_ = bf16[384,256]{1,0:T(8,128)(2,1)S(1)} collective-permute-done((bf16[384,256]{1,0:T(8,128)(2,1)S(1)}, bf16[384,256]{1,0:T(8,128)(2,1)S(1)}, u32[]{:S(2)}, u32[]{:S(2)}) %collective-permute-start.1) | collective-permute-done | bytes 196640 | tf_op jit(solution)/shard_map/ppermute | solution.py:538
  25.5 0.0 collective-permute-start.2
  25.5 3.9 %collective-permute-done.4.refs_1_ = bf16[96,1024]{1,0:T(8,128)(2,1)S(1)} collective-permute-done((bf16[96,1024]{1,0:T(8,128)(2,1)S(1)}, bf16[96,1024]{1,0:T(8,128)(2,1)S(1)}, u32[]{:S(2)}, u32[]{:S(2)}) %collective-permute-start.4) | collective-permute-done | bytes 196640 | tf_op jit(solution)/shard_map/ppermute | solution.py:537
  29.5 0.0 collective-permute-start.5
  29.5 1.9 %shard_map.141 = (f32[4,2,128,256]{3,2,1,0:T(8,128)S(1)}, f32[4,2,8,256]{3,2,1,0:T(8,128)S(1)}, f32[2,128,256]{2,1,0:T(8,128)S(1)}, f32[2,8,256]{2,1,0:T(8,128)S(1)}) custom-call(s32[4]{0:T(128)S(1)} %copy-done.2, bf16[96,1024]{1,0:T(8,128)(2,1)S(1)} %collective-permute-done.4.refs_1_, bf16[384,256]{1,0:T(8,128)(2,1)S(1)} %collective-permute-done.1.refs_2_, ...), custom_call_target="tpu_custom_call" | custom-call | flops 3000000000 | bytes 9000000 | tf_op jit(solution)/shard_map/pallas_call | solution.py:590
  31.4 5.8 %collective-permute-done.5.key_ref = bf16[96,1024]{1,0:T(8,128)(2,1)S(1)} collective-permute-done((bf16[96,1024]{1,0:T(8,128)(2,1)S(1)}, bf16[96,1024]{1,0:T(8,128)(2,1)S(1)}, u32[]{:S(2)}, u32[]{:S(2)}) %collective-permute-start.5) | collective-permute-done | bytes 196640 | tf_op jit(solution)/shard_map/ppermute | solution.py:537
  37.2 1.6 %far.1 = (f32[4,2,256,128]{3,2,1,0:T(8,128)S(1)}, bf16[4,2,256,96]{3,2,1,0:T(8,128)(2,1)S(1)}, f32[2,256,128]{2,1,0:T(8,128)S(1)}, bf16[2,256,384]{2,1,0:T(8,128)(2,1)S(1)}) custom-call(s32[4]{0:T(128)S(1)} %copy-done.2, bf16[96,1024]{1,0:T(8,128)(2,1)S(1)} %collective-permute-done.5.key_ref, f32[2,80,128]{2,1,0:T(8,128)S(1)} %get-tuple-element.19.refs_5_.refs_3_.table_ref, ...), custom_call_target="tpu_custom_call" | custom-call | flops 2000000000 | bytes 6000000 | tf_op jit(solution)/shard_map/far/pallas_call | solution.py:600
  38.8 0.0 collective-permute-done.2.value_ref
  38.8 1.1 %last.1 = (bf16[4,32,2048]{2,1,0:T(8,128)(2,1)}, bf16[8,4,2048]{2,1,0:T(4,128)(2,1)}) custom-call(bf16[384,256]{1,0:T(8,128)(2,1)S(1)} %collective-permute-done.2.value_ref, f32[4,2,256,128]{3,2,1,0:T(8,128)S(1)} %get-tuple-element.32.base_ref, bf16[4,2,256,96]{3,2,1,0:T(8,128)(2,1)S(1)} %get-tuple-element.33.weight_ref, ...), custom_call_target="tpu_custom_call" | custom-call | flops 1000000000 | bytes 3000000 | tf_op jit(solution)/shard_map/last/pallas_call | solution.py:617
  (1 shorter events, 0.0 us)
Async XLA Ops:
  1.7 5.7 %copy-start = (s32[8]{0:T(128)S(1)}, s32[8]{0:T(128)}, u32[]{:S(2)}) copy-start(s32[8]{0:T(128)} %request_ref.1) | copy-start | bytes 100
  1.7 5.7 %copy-start.1 = (s32[8]{0:T(128)S(1)}, s32[8]{0:T(128)}, u32[]{:S(2)}) copy-start(s32[8]{0:T(128)} %length_ref.1) | copy-start | bytes 100
  1.7 5.7 %copy-start.2 = (s32[4]{0:T(128)S(1)}, s32[4]{0:T(128)}, u32[]{:S(2)}) copy-start(s32[4]{0:T(128)} %begin_ref.3) | copy-start | bytes 52
  1.7 14.3 %collective-permute-start.3 = (bf16[96,1024]{1,0:T(8,128)(2,1)S(1)}, bf16[96,1024]{1,0:T(8,128)(2,1)S(1)}, u32[]{:S(2)}, u32[]{:S(2)}) collective-permute-start(bf16[96,1024]{1,0:T(8,128)(2,1)S(1)} %pack_keys.1.after_ref.refs_1_), channel_id=1, source_target_pairs={{0,4},{4,8},{8,12},{12,0},{1,5},{5,9},{9,13},{13,1},{2,6},{6,10},{... | collective-permute-start | bytes 589832 | tf_op jit(solution)/shard_map/ppermute | solution.py:537
  5.8 10.2 %collective-permute-start = (bf16[384,256]{1,0:T(8,128)(2,1)S(1)}, bf16[384,256]{1,0:T(8,128)(2,1)S(1)}, u32[]{:S(2)}, u32[]{:S(2)}) collective-permute-start(bf16[384,256]{1,0:T(8,128)(2,1)S(1)} %pack_values.1.refs_3_), channel_id=1, source_target_pairs={{0,4},{4,8},{8,12},{12,0},{1,5},{5,9},{9,13},{13,1},{2,6},{6,10},{... | collective-permute-start | bytes 589832 | tf_op jit(solution)/shard_map/ppermute | solution.py:538
  16.0 9.6 %collective-permute-start.1 = (bf16[384,256]{1,0:T(8,128)(2,1)S(1)}, bf16[384,256]{1,0:T(8,128)(2,1)S(1)}, u32[]{:S(2)}, u32[]{:S(2)}) collective-permute-start(bf16[384,256]{1,0:T(8,128)(2,1)S(1)} %collective-permute-done.refs_4_), channel_id=1, source_target_pairs={{0,4},{4,8},{8,12},{12,0},{1,5},{5,9},{9,13},{13,1},{2,6},{6,10},{... | collective-permute-start | bytes 589832 | tf_op jit(solution)/shard_map/ppermute | solution.py:538
  16.0 13.5 %collective-permute-start.4 = (bf16[96,1024]{1,0:T(8,128)(2,1)S(1)}, bf16[96,1024]{1,0:T(8,128)(2,1)S(1)}, u32[]{:S(2)}, u32[]{:S(2)}) collective-permute-start(bf16[96,1024]{1,0:T(8,128)(2,1)S(1)} %collective-permute-done.3.refs_2_), channel_id=1, source_target_pairs={{0,4},{4,8},{8,12},{12,0},{1,5},{5,9},{9,13},{13,1},{2,6},{6,10},{... | collective-permute-start | bytes 589832 | tf_op jit(solution)/shard_map/ppermute | solution.py:537
  25.5 13.3 %collective-permute-start.2 = (bf16[384,256]{1,0:T(8,128)(2,1)S(1)}, bf16[384,256]{1,0:T(8,128)(2,1)S(1)}, u32[]{:S(2)}, u32[]{:S(2)}) collective-permute-start(bf16[384,256]{1,0:T(8,128)(2,1)S(1)} %collective-permute-done.1.refs_2_), channel_id=1, source_target_pairs={{0,4},{4,8},{8,12},{12,0},{1,5},{5,9},{9,13},{13,1},{2,6},{6,10},{... | collective-permute-start | bytes 589832 | tf_op jit(solution)/shard_map/ppermute | solution.py:538
  29.5 7.7 %collective-permute-start.5 = (bf16[96,1024]{1,0:T(8,128)(2,1)S(1)}, bf16[96,1024]{1,0:T(8,128)(2,1)S(1)}, u32[]{:S(2)}, u32[]{:S(2)}) collective-permute-start(bf16[96,1024]{1,0:T(8,128)(2,1)S(1)} %collective-permute-done.4.refs_1_), channel_id=1, source_target_pairs={{0,4},{4,8},{8,12},{12,0},{1,5},{5,9},{9,13},{13,1},{2,6},{6,10},{... | collective-permute-start | bytes 589832 | tf_op jit(solution)/shard_map/ppermute | solution.py:537

commit v2 on v1

--- a/solution.py
+++ b/solution.py
@@ -67,6 +67,16 @@
 def first_head(q_heads, kv_local):
     block = lax.axis_index("head") * lax.axis_size("rep") + lax.axis_index("rep")
     return block * q_heads // GROUPS - lax.axis_index("head") * kv_local
+
+
+def ring_order(shards):
+    return [*range(0, shards, 2), *reversed(range(1, shards, 2))]
+
+
+def ring_source(me, shards, hop):
+    place = jnp.where(lax.rem(me, 2) == 0, me // 2, shards - 1 - me // 2)
+    place = lax.rem(place + shards - hop, shards)
+    return jnp.where(place < (shards + 1) // 2, 2 * place, 2 * (shards - 1 - place) + 1)
 
 
 def dot_nt(a, b):
@@ -310,7 +320,7 @@
     size = keys[0].shape[0]
     me = lax.axis_index("seq")
     pre = size - ch
-    shard = [lax.rem(me + shards - hop, shards) for hop in hops]
+    shard = [ring_source(me, shards, hop) for hop in hops]
     for c in range(count):
         rotate_keys(
             keys[c], k_scr, table_ref, shards, prompts, used, pre, ch, shard[c], c * size
@@ -393,7 +403,7 @@
     size = key_ref.shape[0]
     me = lax.axis_index("seq")
     pre = size - ch
-    shard = lax.rem(me + 1, shards)
+    shard = ring_source(me, shards, shards - 1)
     rotate_keys(key_ref, k_scr, table_ref, shards, prompts, used, pre, ch, shard, 0)
     token = me * ch + iota((1, rows), 1) % ch
 
@@ -530,7 +540,8 @@
         name="pack_values",
     )(*in_hbm(prompt_cache_values, span_raw_values), own_keys)
 
-    ring = [(i, (i + 1) % shards) for i in range(shards)]
+    order = ring_order(shards)
+    ring = list(zip(order, order[1:] + order[:1]))
     keys = [own_keys]
     values = [own_values]
     for _ in range(1, shards):

time: 40.2 us -> 36.7 us (0.913)
  waiting for transfers between devices: 19.5 us -> 5.51 us
  starting transfers between devices: 6.03 us -> 16.6 us
    ppermute x3, waiting for transfers between devices: 9.73 us -> 2.13 us  [body(): keys.append(lax.ppermute(keys[-1], 'seq', ring))]
    ppermute x3, starting transfers between devices: 1.63 us -> 8.39 us  [body(): values.append(lax.ppermute(values[-1], 'seq', ring))]
    ppermute x3, waiting for transfers between devices: 9.81 us -> 3.38 us  [body(): values.append(lax.ppermute(values[-1], 'seq', ring))]
    ppermute x3, starting transfers between devices: 4.4 us -> 8.18 us  [body(): keys.append(lax.ppermute(keys[-1], 'seq', ring))]
  transfers between devices with their start and end apart: 6 -> 6, of which waited for: 4 -> 4; matrix products, arithmetic and copies ran while one was open for 0% -> 0% of each run, Pallas kernels for 29% -> 31%
where the time goes in v2:
time: 36.7 us; the launch traced here: 36.4 us
  starting transfers between devices  16.6 us (45%)
  Pallas kernels  13.6 us (37%)
  waiting for transfers between devices  5.51 us (15%)
  between operations  0.71 us (2%)
    ppermute x3, starting transfers between devices, body(): values.append(lax.ppermute(values[-1], 'seq', ring))  8.39 us
    ppermute x3, starting transfers between devices, body(): keys.append(lax.ppermute(keys[-1], 'seq', ring))  8.18 us
    pallas_call x2, Pallas kernels, body(): pl.pallas_call(functools.partial(near_kernel, shards, used, ch, hops), ou...  5.1 us
    pallas_call x1, Pallas kernels, body(): pl.pallas_call(functools.partial(prepare_kernel, shards, q_heads, kv_loca...  3.8 us
    ppermute x3, waiting for transfers between devices, body(): values.append(lax.ppermute(values[-1], 'seq', ring))  3.38 us
    ppermute x3, waiting for transfers between devices, body(): keys.append(lax.ppermute(keys[-1], 'seq', ring))  2.13 us
    pallas_call x1, Pallas kernels, body(): pl.pallas_call(functools.partial(far_kernel, shards, used, ch), out_shape...  1.63 us
    pallas_call x1, Pallas kernels, body(): pl.pallas_call(functools.partial(last_kernel, used, per_kv, steps), out_s...  1.09 us
  transfers between devices with their start and end apart: 6, of which 4 were waited for; matrix products, arithmetic and copies ran while one was open for 0% of the time, Pallas kernels for 31%

profile of v2, /device:TPU:0, one launch (start us, length us, event | category | flops | bytes accessed | tf_op | source)
XLA Modules:
  0.0 36.4 jit_solution(7601647610593183993)
XLA Ops:
  0.6 1.0 %pack_keys.1.after_ref.refs_1_ = bf16[96,1024]{1,0:T(8,128)(2,1)S(1)} custom-call(bf16[4,64,512]{2,1,0:T(8,128)(2,1)} %cache_ref.2, bf16[4,32,512]{2,1,0:T(8,128)(2,1)} %span_ref.2), custom_call_target="tpu_custom_call" | custom-call | flops 1000000000 | bytes 3000000 | tf_op jit(solution)/shard_map/pack_keys/pallas_call | solution.py:522
  1.7 0.0 copy-start
  1.7 0.0 copy-start.1
  1.7 0.0 copy-start.2
  1.7 4.1 %collective-permute-start.3 = (bf16[96,1024]{1,0:T(8,128)(2,1)S(1)}, bf16[96,1024]{1,0:T(8,128)(2,1)S(1)}, u32[]{:S(2)}, u32[]{:S(2)}) collective-permute-start(bf16[96,1024]{1,0:T(8,128)(2,1)S(1)} %pack_keys.1.after_ref.refs_1_), channel_id=1, source_target_pairs={{0,8},{8,12},{12,4},{4,0},{1,9},{9,13},{13,5},{5,1},{2,10},{10,14}... | collective-permute-start | bytes 589832 | tf_op jit(solution)/shard_map/ppermute | solution.py:548
  5.8 0.9 %pack_values.1.refs_3_ = bf16[384,256]{1,0:T(8,128)(2,1)S(1)} custom-call(bf16[4,64,512]{2,1,0:T(8,128)(2,1)} %cache_ref.3, bf16[4,32,512]{2,1,0:T(8,128)(2,1)} %span_ref.3, bf16[96,1024]{1,0:T(8,128)(2,1)S(1)} %pack_keys.1.after_ref.refs_1_), custom_call_target="tpu_custom_call" | custom-call | flops 1000000000 | bytes 3000000 | tf_op jit(solution)/shard_map/pack_values/pallas_call | solution.py:532
  6.8 1.6 %collective-permute-start = (bf16[384,256]{1,0:T(8,128)(2,1)S(1)}, bf16[384,256]{1,0:T(8,128)(2,1)S(1)}, u32[]{:S(2)}, u32[]{:S(2)}) collective-permute-start(bf16[384,256]{1,0:T(8,128)(2,1)S(1)} %pack_values.1.refs_3_), channel_id=1, source_target_pairs={{0,8},{8,12},{12,4},{4,0},{1,9},{9,13},{13,5},{5,1},{2,10},{10,14}... | collective-permute-start | bytes 589832 | tf_op jit(solution)/shard_map/ppermute | solution.py:549
  8.4 0.0 copy-done
  8.4 0.0 copy-done.2
  8.4 3.8 %prepare.1 = (f32[2,80,128]{2,1,0:T(8,128)S(1)}, bf16[4,2,256,128]{3,2,1,0:T(8,128)(2,1)S(1)}, bf16[2,256,512]{2,1,0:T(8,128)(2,1)S(1)}, f32[2,128,256]{2,1,0:T(8,128)S(1)}, f32[2,8,256]{2,1,0:T(8,128)S(1)}) custom-call(s32[4]{0:T(128)S(1)} %copy-done.2, s32[8]{0:T(128)S(1)} %copy-done, s32[8]{0:T(128)S(1)} %copy-done.1, bf16[4,32,2048]{2,1,0:T(8,128)(2,1)} %span_q_ref.1, ...), custom_call_target="tpu_custom_call" | custom-call | flops 3000000000 | bytes 9000000 | tf_op jit(solution)/shard_map/prepare/pallas_call | solution.py:552
  12.2 2.0 %collective-permute-done.refs_4_ = bf16[384,256]{1,0:T(8,128)(2,1)S(1)} collective-permute-done((bf16[384,256]{1,0:T(8,128)(2,1)S(1)}, bf16[384,256]{1,0:T(8,128)(2,1)S(1)}, u32[]{:S(2)}, u32[]{:S(2)}) %collective-permute-start) | collective-permute-done | bytes 196640 | tf_op jit(solution)/shard_map/ppermute | solution.py:549
  14.2 3.4 %collective-permute-start.1 = (bf16[384,256]{1,0:T(8,128)(2,1)S(1)}, bf16[384,256]{1,0:T(8,128)(2,1)S(1)}, u32[]{:S(2)}, u32[]{:S(2)}) collective-permute-start(bf16[384,256]{1,0:T(8,128)(2,1)S(1)} %collective-permute-done.refs_4_), channel_id=1, source_target_pairs={{0,8},{8,12},{12,4},{4,0},{1,9},{9,13},{13,5},{5,1},{2,10},{10,14}... | collective-permute-start | bytes 589832 | tf_op jit(solution)/shard_map/ppermute | solution.py:549
  17.6 0.0 collective-permute-done.3.refs_2_
  17.6 0.7 %collective-permute-start.4 = (bf16[96,1024]{1,0:T(8,128)(2,1)S(1)}, bf16[96,1024]{1,0:T(8,128)(2,1)S(1)}, u32[]{:S(2)}, u32[]{:S(2)}) collective-permute-start(bf16[96,1024]{1,0:T(8,128)(2,1)S(1)} %collective-permute-done.3.refs_2_), channel_id=1, source_target_pairs={{0,8},{8,12},{12,4},{4,0},{1,9},{9,13},{13,5},{5,1},{2,10},{10,14}... | collective-permute-start | bytes 589832 | tf_op jit(solution)/shard_map/ppermute | solution.py:548
  18.3 3.2 %shard_map.140 = (f32[4,2,128,256]{3,2,1,0:T(8,128)S(1)}, f32[4,2,8,256]{3,2,1,0:T(8,128)S(1)}, f32[2,128,256]{2,1,0:T(8,128)S(1)}, f32[2,8,256]{2,1,0:T(8,128)S(1)}) custom-call(s32[4]{0:T(128)S(1)} %copy-done.2, bf16[96,1024]{1,0:T(8,128)(2,1)S(1)} %pack_keys.1.after_ref.refs_1_, bf16[96,1024]{1,0:T(8,128)(2,1)S(1)} %collective-permute-done.3.refs_2_, ...), custom_call_target="tpu_custom_call" | custom-call | flops 3000000000 | bytes 9000000 | tf_op jit(solution)/shard_map/pallas_call | solution.py:601
  21.5 1.4 %collective-permute-done.1.refs_2_ = bf16[384,256]{1,0:T(8,128)(2,1)S(1)} collective-permute-done((bf16[384,256]{1,0:T(8,128)(2,1)S(1)}, bf16[384,256]{1,0:T(8,128)(2,1)S(1)}, u32[]{:S(2)}, u32[]{:S(2)}) %collective-permute-start.1) | collective-permute-done | bytes 196640 | tf_op jit(solution)/shard_map/ppermute | solution.py:549
  22.9 3.4 %collective-permute-start.2 = (bf16[384,256]{1,0:T(8,128)(2,1)S(1)}, bf16[384,256]{1,0:T(8,128)(2,1)S(1)}, u32[]{:S(2)}, u32[]{:S(2)}) collective-permute-start(bf16[384,256]{1,0:T(8,128)(2,1)S(1)} %collective-permute-done.1.refs_2_), channel_id=1, source_target_pairs={{0,8},{8,12},{12,4},{4,0},{1,9},{9,13},{13,5},{5,1},{2,10},{10,14}... | collective-permute-start | bytes 589832 | tf_op jit(solution)/shard_map/ppermute | solution.py:549
  26.3 0.8 %collective-permute-done.4.refs_1_ = bf16[96,1024]{1,0:T(8,128)(2,1)S(1)} collective-permute-done((bf16[96,1024]{1,0:T(8,128)(2,1)S(1)}, bf16[96,1024]{1,0:T(8,128)(2,1)S(1)}, u32[]{:S(2)}, u32[]{:S(2)}) %collective-permute-start.4) | collective-permute-done | bytes 196640 | tf_op jit(solution)/shard_map/ppermute | solution.py:548
  27.1 3.4 %collective-permute-start.5 = (bf16[96,1024]{1,0:T(8,128)(2,1)S(1)}, bf16[96,1024]{1,0:T(8,128)(2,1)S(1)}, u32[]{:S(2)}, u32[]{:S(2)}) collective-permute-start(bf16[96,1024]{1,0:T(8,128)(2,1)S(1)} %collective-permute-done.4.refs_1_), channel_id=1, source_target_pairs={{0,8},{8,12},{12,4},{4,0},{1,9},{9,13},{13,5},{5,1},{2,10},{10,14}... | collective-permute-start | bytes 589832 | tf_op jit(solution)/shard_map/ppermute | solution.py:548
  30.5 1.9 %shard_map.141 = (f32[4,2,128,256]{3,2,1,0:T(8,128)S(1)}, f32[4,2,8,256]{3,2,1,0:T(8,128)S(1)}, f32[2,128,256]{2,1,0:T(8,128)S(1)}, f32[2,8,256]{2,1,0:T(8,128)S(1)}) custom-call(s32[4]{0:T(128)S(1)} %copy-done.2, bf16[96,1024]{1,0:T(8,128)(2,1)S(1)} %collective-permute-done.4.refs_1_, bf16[384,256]{1,0:T(8,128)(2,1)S(1)} %collective-permute-done.1.refs_2_, ...), custom_call_target="tpu_custom_call" | custom-call | flops 3000000000 | bytes 9000000 | tf_op jit(solution)/shard_map/pallas_call | solution.py:601
  32.4 1.3 %collective-permute-done.5.key_ref = bf16[96,1024]{1,0:T(8,128)(2,1)S(1)} collective-permute-done((bf16[96,1024]{1,0:T(8,128)(2,1)S(1)}, bf16[96,1024]{1,0:T(8,128)(2,1)S(1)}, u32[]{:S(2)}, u32[]{:S(2)}) %collective-permute-start.5) | collective-permute-done | bytes 196640 | tf_op jit(solution)/shard_map/ppermute | solution.py:548
  33.7 1.6 %far.1 = (f32[4,2,256,128]{3,2,1,0:T(8,128)S(1)}, bf16[4,2,256,96]{3,2,1,0:T(8,128)(2,1)S(1)}, f32[2,256,128]{2,1,0:T(8,128)S(1)}, bf16[2,256,384]{2,1,0:T(8,128)(2,1)S(1)}) custom-call(s32[4]{0:T(128)S(1)} %copy-done.2, bf16[96,1024]{1,0:T(8,128)(2,1)S(1)} %collective-permute-done.5.key_ref, f32[2,80,128]{2,1,0:T(8,128)S(1)} %get-tuple-element.19.refs_5_.refs_3_.table_ref, ...), custom_call_target="tpu_custom_call" | custom-call | flops 2000000000 | bytes 6000000 | tf_op jit(solution)/shard_map/far/pallas_call | solution.py:611
  35.3 0.0 collective-permute-done.2.value_ref
  35.3 1.1 %last.1 = (bf16[4,32,2048]{2,1,0:T(8,128)(2,1)}, bf16[8,4,2048]{2,1,0:T(4,128)(2,1)}) custom-call(bf16[384,256]{1,0:T(8,128)(2,1)S(1)} %collective-permute-done.2.value_ref, f32[4,2,256,128]{3,2,1,0:T(8,128)S(1)} %get-tuple-element.32.base_ref, bf16[4,2,256,96]{3,2,1,0:T(8,128)(2,1)S(1)} %get-tuple-element.33.weight_ref, ...), custom_call_target="tpu_custom_call" | custom-call | flops 1000000000 | bytes 3000000 | tf_op jit(solution)/shard_map/last/pallas_call | solution.py:628
  (1 shorter events, 0.0 us)
Async XLA Ops:
  1.7 6.7 %copy-start = (s32[8]{0:T(128)S(1)}, s32[8]{0:T(128)}, u32[]{:S(2)}) copy-start(s32[8]{0:T(128)} %request_ref.1) | copy-start | bytes 100
  1.7 6.7 %copy-start.1 = (s32[8]{0:T(128)S(1)}, s32[8]{0:T(128)}, u32[]{:S(2)}) copy-start(s32[8]{0:T(128)} %length_ref.1) | copy-start | bytes 100
  1.7 6.7 %copy-start.2 = (s32[4]{0:T(128)S(1)}, s32[4]{0:T(128)}, u32[]{:S(2)}) copy-start(s32[4]{0:T(128)} %begin_ref.3) | copy-start | bytes 52
  1.7 15.9 %collective-permute-start.3 = (bf16[96,1024]{1,0:T(8,128)(2,1)S(1)}, bf16[96,1024]{1,0:T(8,128)(2,1)S(1)}, u32[]{:S(2)}, u32[]{:S(2)}) collective-permute-start(bf16[96,1024]{1,0:T(8,128)(2,1)S(1)} %pack_keys.1.after_ref.refs_1_), channel_id=1, source_target_pairs={{0,8},{8,12},{12,4},{4,0},{1,9},{9,13},{13,5},{5,1},{2,10},{10,14}... | collective-permute-start | bytes 589832 | tf_op jit(solution)/shard_map/ppermute | solution.py:548
  6.8 7.4 %collective-permute-start = (bf16[384,256]{1,0:T(8,128)(2,1)S(1)}, bf16[384,256]{1,0:T(8,128)(2,1)S(1)}, u32[]{:S(2)}, u32[]{:S(2)}) collective-permute-start(bf16[384,256]{1,0:T(8,128)(2,1)S(1)} %pack_values.1.refs_3_), channel_id=1, source_target_pairs={{0,8},{8,12},{12,4},{4,0},{1,9},{9,13},{13,5},{5,1},{2,10},{10,14}... | collective-permute-start | bytes 589832 | tf_op jit(solution)/shard_map/ppermute | solution.py:549
  14.2 8.7 %collective-permute-start.1 = (bf16[384,256]{1,0:T(8,128)(2,1)S(1)}, bf16[384,256]{1,0:T(8,128)(2,1)S(1)}, u32[]{:S(2)}, u32[]{:S(2)}) collective-permute-start(bf16[384,256]{1,0:T(8,128)(2,1)S(1)} %collective-permute-done.refs_4_), channel_id=1, source_target_pairs={{0,8},{8,12},{12,4},{4,0},{1,9},{9,13},{13,5},{5,1},{2,10},{10,14}... | collective-permute-start | bytes 589832 | tf_op jit(solution)/shard_map/ppermute | solution.py:549
  17.6 9.5 %collective-permute-start.4 = (bf16[96,1024]{1,0:T(8,128)(2,1)S(1)}, bf16[96,1024]{1,0:T(8,128)(2,1)S(1)}, u32[]{:S(2)}, u32[]{:S(2)}) collective-permute-start(bf16[96,1024]{1,0:T(8,128)(2,1)S(1)} %collective-permute-done.3.refs_2_), channel_id=1, source_target_pairs={{0,8},{8,12},{12,4},{4,0},{1,9},{9,13},{13,5},{5,1},{2,10},{10,14}... | collective-permute-start | bytes 589832 | tf_op jit(solution)/shard_map/ppermute | solution.py:548
  22.9 12.4 %collective-permute-start.2 = (bf16[384,256]{1,0:T(8,128)(2,1)S(1)}, bf16[384,256]{1,0:T(8,128)(2,1)S(1)}, u32[]{:S(2)}, u32[]{:S(2)}) collective-permute-start(bf16[384,256]{1,0:T(8,128)(2,1)S(1)} %collective-permute-done.1.refs_2_), channel_id=1, source_target_pairs={{0,8},{8,12},{12,4},{4,0},{1,9},{9,13},{13,5},{5,1},{2,10},{10,14}... | collective-permute-start | bytes 589832 | tf_op jit(solution)/shard_map/ppermute | solution.py:549
  27.1 6.6 %collective-permute-start.5 = (bf16[96,1024]{1,0:T(8,128)(2,1)S(1)}, bf16[96,1024]{1,0:T(8,128)(2,1)S(1)}, u32[]{:S(2)}, u32[]{:S(2)}) collective-permute-start(bf16[96,1024]{1,0:T(8,128)(2,1)S(1)} %collective-permute-done.4.refs_1_), channel_id=1, source_target_pairs={{0,8},{8,12},{12,4},{4,0},{1,9},{9,13},{13,5},{5,1},{2,10},{10,14}... | collective-permute-start | bytes 589832 | tf_op jit(solution)/shard_map/ppermute | solution.py:548
